TPU v7x, 256 devices: a whole 4x4x8 slice. The times are simulated.
256 devices in a mesh: prow: 16 (over x, y), pcol: 16 (over z, core).
Axes of the slice: x: 4, y: 4, z: 8, core: 2. Of those that a mesh axis runs over, the one named last changes fastest.
Arguments:
- ainv: float32 [16384, 16384], P('prow', 'pcol'), as said below
- panels: float32 [3, 16384, 512], P(None, 'prow', 'pcol'), may hold values from -0.53 to 0.53
- pattern: int32 [3, 128], replicated, may hold values 0 or 1
- coupling: float32 [3, 512, 512], replicated, may hold values from -0.25 to 0.25
- dinv: float32 [3, 512, 512], replicated, as said below
Outputs:
- xpanel: float32 [3, 16384, 512], P(None, 'prow', 'pcol')
- xcross: float32 [3, 512, 512], P(None, 'pcol')
- ydiag: float32 [3, 512, 512], P(None, 'pcol')
Inputs may be any that keep to these rules, and one draw needn't show every extreme that they name: ainv is symmetric: ainv equals its transpose up to rounding. Each dinv[k] is symmetric: it equals its transpose exactly.
All inputs are finite; a program needn't handle non-finite values.
Results may differ from a plain program's by a relative error of at most 0.000092.
Values sent between devices are 32-bit elements; how exact they have to be, the bound alone decides.
A program may use at most 128 MiB of HBM per device.

v0:
```python
import jax
import jax.numpy as jnp
from jax import lax
from jax.sharding import PartitionSpec as P

NB = 128
high = lax.Precision.HIGH
highest = lax.Precision.HIGHEST


def mm(left, right, precision=high):
    return jnp.dot(left, right, precision=precision, preferred_element_type=jnp.float32)


def tmm(left, right, precision=high):
    return lax.dot_general(
        left,
        right,
        (((0,), (0,)), ((), ())),
        precision=precision,
        preferred_element_type=jnp.float32,
    )


def mmt(left, right, precision=high):
    return lax.dot_general(
        left,
        right,
        (((1,), (1,)), ((), ())),
        precision=precision,
        preferred_element_type=jnp.float32,
    )


def shards(ainv, panels, pattern, coupling, dinv):
    rows = lax.axis_size("prow")
    cols = lax.axis_size("pcol")
    row_index = lax.axis_index("prow")
    col_index = lax.axis_index("pcol")
    count, depth, width = panels.shape
    blocks_here = depth // NB
    flags = lax.dynamic_slice_in_dim(pattern, row_index * blocks_here, blocks_here, 1)
    row_mask = jnp.repeat(flags.astype(jnp.float32), NB, axis=1)
    factors = jnp.swapaxes(panels, 1, 2) * row_mask[:, None, :]
    f0, f1, f2 = lax.all_gather(factors, "pcol", axis=1, tiled=True)
    c0, c1, c2 = (coupling[0], coupling[1], coupling[2])
    u01 = -c0
    u12 = -c2
    u02 = mm(c0, c2, highest) - c1
    h0 = f0
    h1 = f1 + tmm(u01, f0)
    h2 = f2 + tmm(u02, f0) + tmm(u12, f1)
    ht = jnp.concatenate([h0, h1, h2], 0)
    partial = mm(ht, ainv).reshape(count, rows, width, depth)
    mine = lax.psum_scatter(partial, "prow", scatter_dimension=1, tiled=False)
    perm = [(r * cols + c, c * cols + r) for r in range(rows) for c in range(cols)]
    xt = -lax.ppermute(mine, ("prow", "pcol"), perm)
    inner0 = mmt(xt[0], ht)
    inner1 = mmt(xt[1], ht[512:])
    inner2 = mmt(xt[2], ht[1024:])
    summed = lax.psum(jnp.concatenate([inner0, inner1, inner2], 1), "prow")
    start = col_index * width

    def own(matrix, axis):
        return lax.dynamic_slice_in_dim(matrix, start, width, axis)

    d0 = own(dinv[0], 0)
    a01 = tmm(own(u01, 1), dinv[0], highest)
    a02 = tmm(own(u02, 1), dinv[0], highest)
    b1 = own(dinv[1], 0)
    b12 = tmm(own(u12, 1), dinv[1], highest)
    y0 = d0 - summed[:, 0:512]
    e01 = mm(d0, u01, highest) - summed[:, 512:1024]
    e02 = mm(d0, u02, highest) - summed[:, 1024:1536]
    y1 = b1 + mm(a01, u01, highest) - summed[:, 1536:2048]
    e12 = mm(a01, u02, highest) + mm(b1, u12, highest) - summed[:, 2048:2560]
    y2 = own(dinv[2], 0) + mm(a02, u02, highest) + mm(b12, u12, highest) - summed[:, 2560:3072]
    return (jnp.swapaxes(xt, 1, 2), jnp.stack([e01, e02, e12], 0), jnp.stack([y0, y1, y2], 0))


def solution(mesh):
    placed = (P("prow", "pcol"), P(None, "prow", "pcol"), P(), P(), P())
    return jax.shard_map(
        shards,
        mesh=mesh,
        in_specs=placed,
        out_specs=(P(None, "prow", "pcol"), P(None, "pcol", None), P(None, "pcol", None)),
        check_vma=False,
    )
```

profile of v0, /device:TPU:2, one launch (start us, length us, event | category | flops | bytes accessed | tf_op | source)
XLA Modules:
  0.0 337.9 jit_solution(12168469248919959419)
XLA Ops:
  7.2 0.0 slice-start
  7.2 0.0 all-gather.2.cloned.1.call-start
  7.2 0.8 dynamic-slice_convert_fusion
  8.1 0.1 broadcast_bitcast_fusion
  8.1 1.8 multiply_bitcast_fusion
  9.9 0.0 all-gather.2.cloned.1.call-update
  10.0 0.0 reduce-scatter.4.cloned.1.call-start
  10.0 0.0 slice-done
  10.0 1.3 copy.12
  11.3 4.8 %convolution_subtract_fusion = f32[512,512]{0,1:T(8,128)} fusion(f32[1,512,512]{1,2,0:T(8,128)} %copy.12, f32[3,512,512]{2,1,0:T(8,128)} %param.8), kind=kOutput, calls=%fused_computation.14 | convolution fusion | flops 1610874880 | bytes 4194304 | tf_op jit(solution)/shard_map/dot_general | solution.py:12
  16.1 43.3 %all-gather.2.cloned.1.call-done = f32[3,512,1024]{2,1,0:T(8,128)} async-done(((f32[3,32,1024]{2,1,0:T(8,128)}), f32[3,512,1024]{2,1,0:T(8,128)}) %all-gather.2.cloned.1.call-update) | async-done | bytes 6291472 | tf_op jit(solution)/shard_map/all_gather | solution.py:45
  59.4 0.0 copy-done
  59.4 4.3 %bitcast_add_fusion = f32[512,1024]{1,0:T(8,128)S(1)} fusion(f32[3,512,1024]{2,1,0:T(8,128)} %all-gather.2.cloned.1.call-done, f32[3,512,512]{2,1,0:T(8,128)S(1)} %copy-done), kind=kOutput, calls=%fused_computation.12 | convolution fusion | flops 1611399168 | bytes 7340032 | tf_op jit(solution)/shard_map/dot_general | solution.py:16
  63.7 0.0 copy-start.6
  63.7 4.0 %slice_bitcast_fusion.2 = f32[512,1024]{1,0:T(8,128)} fusion(f32[3,512,1024]{2,1,0:T(8,128)} %all-gather.2.cloned.1.call-done), kind=kLoop, calls=%fused_computation.11 | loop fusion | bytes 4194304 | tf_op jit(solution)/shard_map/unstack | solution.py:45
  67.7 1.9 fusion.62
  69.7 2.0 fusion.7
  71.8 16.0 %fusion.1 = f32[1536,1024]{1,0:T(8,128)S(1)} fusion(f32[1024,1024]{1,0:T(8,128)} %param.5, f32[512,1024]{1,0:T(8,128)S(1)} %fusion.7, f32[512,1024]{1,0:T(8,128)S(1)} %bitcast_add_fusion, f32[512,1024]{1,0:T(8,128)} %slice_bitcast_fusion.2), kind=kOutput, calls=%fused_computation.2 | convolution fusion | flops 9666822144 | bytes 16777216 | tf_op jit(solution)/shard_map/dot_general | solution.py:12
  87.8 0.0 copy-done.3
  87.8 3.2 copy.11
  91.0 0.0 reduce-scatter.4.cloned.1.call-update
  91.1 0.0 all-reduce.3.cloned.1.call-start
  91.1 0.0 copy-start.2
  91.1 1.3 bitcast_negate_fusion
  92.4 2.0 fusion.21
  94.4 1.0 fusion.65
  95.4 81.0 %reduce-scatter.4.cloned.1.call-done = f32[3,1,32,1024]{3,2,0,1:T(8,128)} async-done(((f32[3,16,32,1024]{3,2,0,1:T(8,128)}), f32[3,1,32,1024]{3,2,0,1:T(8,128)}) %reduce-scatter.4.cloned.1.call-update) | async-done | bytes 393232
  176.5 5.0 %collective-permute-start = (f32[3,32,1024]{2,1,0:T(8,128)}, f32[3,32,1024]{2,1,0:T(8,128)S(1)}, u32[]{:S(2)}, u32[]{:S(2)}) collective-permute-start(f32[3,32,1024]{2,1,0:T(8,128)} %bitcast.108), channel_id=1, source_target_pairs={{0,0},{1,16},{2,32},{3,48},{4,64},{5,80},{6,96},{7,112},{8,128},{9... | collective-permute-start | bytes 1179656 | tf_op jit(solution)/shard_map/ppermute | solution.py:57
  181.4 2.0 fusion.19
  183.4 3.7 %fusion.63 = (f32[1,512,512]{2,1,0:T(8,128)}, f32[1,512,512]{2,1,0:T(8,128)}, f32[1,512,512]{2,1,0:T(8,128)}) fusion(f32[3,512,512]{2,1,0:T(8,128)} %param.9), kind=kLoop, calls=%fused_computation.89 | loop fusion | bytes 6291456 | tf_op jit(solution)/shard_map/slice | solution.py:77
  187.2 29.7 %collective-permute-done = f32[3,32,1024]{2,1,0:T(8,128)S(1)} collective-permute-done((f32[3,32,1024]{2,1,0:T(8,128)}, f32[3,32,1024]{2,1,0:T(8,128)S(1)}, u32[]{:S(2)}, u32[]{:S(2)}) %collective-permute-start) | collective-permute-done | bytes 393248 | tf_op jit(solution)/shard_map/ppermute | solution.py:57
  216.8 0.8 fusion.64
  217.6 0.0 copy-done.8
  217.6 3.0 fusion
  220.6 2.0 fusion.2
  222.6 1.1 fusion.41
  223.7 0.8 pad_maximum_fusion.3
  224.5 0.0 all-reduce.3.cloned.1.call-update
  224.5 2.1 fusion.17
  226.6 2.3 convolution_add_fusion.1
  228.8 92.2 %all-reduce.3.cloned.1.call-done = f32[32,3072]{1,0:T(8,128)} async-done(((f32[32,3072]{1,0:T(8,128)}), f32[32,3072]{1,0:T(8,128)}) %all-reduce.3.cloned.1.call-update) | async-done | bytes 393232 | tf_op jit(solution)/shard_map/psum | solution.py:61
  321.0 2.3 fusion.15
  323.3 1.6 fusion.16
  324.9 0.9 fusion.42
  325.8 1.6 fusion.12
  327.4 1.6 fusion.14
  329.0 1.6 fusion.10
  330.6 0.8 pad_maximum_fusion.4
  (14 shorter events, 0.0 us)
Async XLA Ops:
  7.2 2.8 slice-start
  7.2 52.3 %all-gather.2.cloned.1.call-start = ((), (), s32[]{:S(2)}) async-start(), calls=%async_computation.1 | async-start | bytes 6684672 | tf_op jit(solution)/shard_map/all_gather | solution.py:45
  10.0 166.5 %reduce-scatter.4.cloned.1.call-start = ((), (), s32[]{:S(2)}) async-start(), calls=%async_computation.3 | async-start | bytes 6684672
  11.3 48.1 %copy-start = (f32[3,512,512]{2,1,0:T(8,128)S(1)}, f32[3,512,512]{2,1,0:T(8,128)}, u32[]{:S(2)}) copy-start(f32[3,512,512]{2,1,0:T(8,128)} %param.8) | copy-start | bytes 9437188
  59.4 8.3 %copy-start.5 = (f32[3,512,1024]{2,1,0:T(8,128)S(1)}, f32[3,512,1024]{2,1,0:T(8,128)}, u32[]{:S(2)}) copy-start(f32[3,512,1024]{2,1,0:T(8,128)} %all-gather.2.cloned.1.call-done) | copy-start | bytes 18874372
  63.7 8.0 %copy-start.6 = (f32[512,1024]{1,0:T(8,128)}, f32[512,1024]{1,0:T(8,128)S(1)}, u32[]{:S(2)}) copy-start(f32[512,1024]{1,0:T(8,128)S(1)} %bitcast_add_fusion) | copy-start | bytes 6291460
  63.7 4.0 %copy-start.1 = (f32[512,512]{0,1:T(8,128)S(1)}, f32[512,512]{0,1:T(8,128)}, u32[]{:S(2)}) copy-start(f32[512,512]{0,1:T(8,128)} %convolution_subtract_fusion) | copy-start | bytes 3145732
  71.7 16.0 %copy-start.3 = (f32[512,1024]{1,0:T(8,128)}, f32[512,1024]{1,0:T(8,128)S(1)}, u32[]{:S(2)}) copy-start(f32[512,1024]{1,0:T(8,128)S(1)} %fusion.7) | copy-start | bytes 6291460
  91.1 229.9 %all-reduce.3.cloned.1.call-start = ((), (), s32[]{:S(2)}) async-start(), calls=%async_computation.2 | async-start | bytes 786432 | tf_op jit(solution)/shard_map/psum | solution.py:61
  91.1 3.2 copy-start.2
  176.5 40.4 %collective-permute-start = (f32[3,32,1024]{2,1,0:T(8,128)}, f32[3,32,1024]{2,1,0:T(8,128)S(1)}, u32[]{:S(2)}, u32[]{:S(2)}) collective-permute-start(f32[3,32,1024]{2,1,0:T(8,128)} %bitcast.108), channel_id=1, source_target_pairs={{0,0},{1,16},{2,32},{3,48},{4,64},{5,80},{6,96},{7,112},{8,128},{9... | collective-permute-start | bytes 1179656 | tf_op jit(solution)/shard_map/ppermute | solution.py:57
  183.4 34.2 %copy-start.4 = (f32[512,1024]{1,0:T(8,128)S(1)}, f32[512,1024]{1,0:T(8,128)}, u32[]{:S(2)}) copy-start(f32[512,1024]{1,0:T(8,128)} %copy-done.3) | copy-start | bytes 6291460
  183.4 34.2 %copy-start.7 = (f32[512,1024]{1,0:T(8,128)S(1)}, f32[512,1024]{1,0:T(8,128)}, u32[]{:S(2)}) copy-start(f32[512,1024]{1,0:T(8,128)} %copy-done.6) | copy-start | bytes 6291460
  183.4 34.2 %copy-start.8 = (f32[512,1024]{1,0:T(8,128)S(1)}, f32[512,1024]{1,0:T(8,128)}, u32[]{:S(2)}) copy-start(f32[512,1024]{1,0:T(8,128)} %slice_bitcast_fusion.2) | copy-start | bytes 6291460
Sparse Core Ops, SparseCore 0:
  10.4 48.9 all-gather.1
  91.2 85.2 reduce-scatter.3
  224.6 96.3 all-reduce.2
where the time goes:
time: 338 us
  waiting for transfers between devices  246 us (73%)
  matrix products  53.1 us (16%)
  between operations  14 us (4%)
  local copies, waits for them, and re-layouts  12.4 us (4%)
  other arithmetic  7.1 us (2%)
  starting transfers between devices  5.08 us (2%)
    psum x1, waiting for transfers between devices, shards(): summed = lax.psum(jnp.concatenate([inner0, inner1, inner2], 1), 'prow')  92.2 us
    unnamed x4, waiting for transfers between devices  81.1 us
    all_gather x1, waiting for transfers between devices, shards(): f0, f1, f2 = lax.all_gather(factors, 'pcol', axis=1, tiled=True)  43.3 us
    dot_general x9, matrix products, mm(): jnp.dot(left, right, precision=precision, preferred_element_type=jnp.floa...  32.8 us
    ppermute x1, waiting for transfers between devices, shards(): xt = -lax.ppermute(mine, ('prow', 'pcol'), perm)  29.7 us
    dot_general x6, matrix products, tmm(): lax.dot_general(left, right, (((0,), (0,)), ((), ())), precision=precisio...  14.2 us
  transfers between devices with their start and end apart: 4, of which 4 were waited for; matrix products, arithmetic and copies ran while one was open for 6% of the time, Pallas kernels for 0%

commit v1 on v0

--- a/solution.py
+++ b/solution.py
@@ -6,6 +6,13 @@
 NB = 128
 high = lax.Precision.HIGH
 highest = lax.Precision.HIGHEST
+
+
+def swapped_in(x, axis, dim):
+    size = lax.axis_size(axis)
+    shards = jnp.stack([x for _ in range(size)])
+    shards = lax.all_to_all(shards, axis, split_axis=0, concat_axis=0)
+    return jnp.concatenate(shards, axis=dim)
 
 
 def mm(left, right, precision=high):
@@ -42,7 +49,7 @@
     flags = lax.dynamic_slice_in_dim(pattern, row_index * blocks_here, blocks_here, 1)
     row_mask = jnp.repeat(flags.astype(jnp.float32), NB, axis=1)
     factors = jnp.swapaxes(panels, 1, 2) * row_mask[:, None, :]
-    f0, f1, f2 = lax.all_gather(factors, "pcol", axis=1, tiled=True)
+    f0, f1, f2 = swapped_in(factors, "pcol", 1)
     c0, c1, c2 = (coupling[0], coupling[1], coupling[2])
     u01 = -c0
     u12 = -c2

time: 338 us -> 434 us (1.28)
  waiting for transfers between devices: 246 us -> 338 us
  starting transfers between devices: 5.08 us -> 13.8 us
  matrix products: 53.1 us -> 45.3 us
    all_to_all x0 -> x1, waiting for transfers between devices: none -> 134 us  [swapped_in(): shards = lax.all_to_all(shards, axis, split_axis=0, concat_axis=0)]
    all_gather x1 -> x0, waiting for transfers between devices: 43.3 us -> none  [shards(): f0, f1, f2 = lax.all_gather(factors, 'pcol', axis=1, tiled=True)]
    all_to_all x0 -> x1, starting transfers between devices: none -> 8.75 us  [swapped_in(): shards = lax.all_to_all(shards, axis, split_axis=0, concat_axis=0)]
    dot_general x9, matrix products: 32.8 us -> 27.3 us  [mm(): jnp.dot(left, right, precision=precision, preferred_element_type=jnp.floa...]
    unnamed x4 -> x3, waiting for transfers between devices: 81.1 us -> 81.5 us
  transfers between devices with their start and end apart: 4 -> 4, of which waited for: 4 -> 4; matrix products, arithmetic and copies ran while one was open for 6% -> 4% of each run, Pallas kernels for 0% -> 0%
where the time goes in v1:
time: 434 us; the launch traced here: 433 us
  waiting for transfers between devices  338 us (78%)
  matrix products  45.3 us (10%)
  local copies, waits for them, and re-layouts  15.9 us (4%)
  between operations  14.3 us (3%)
  starting transfers between devices  13.8 us (3%)
  other arithmetic  6.24 us (1%)
    all_to_all x1, waiting for transfers between devices, swapped_in(): shards = lax.all_to_all(shards, axis, split_axis=0, concat_axis=0)  134 us
    psum x1, waiting for transfers between devices, shards(): summed = lax.psum(jnp.concatenate([inner0, inner1, inner2], 1), 'prow')  92.2 us
    unnamed x3, waiting for transfers between devices  81.5 us
    ppermute x1, waiting for transfers between devices, shards(): xt = -lax.ppermute(mine, ('prow', 'pcol'), perm)  29.7 us
    dot_general x9, matrix products, mm(): jnp.dot(left, right, precision=precision, preferred_element_type=jnp.floa...  27.3 us
    dot_general x6, matrix products, tmm(): lax.dot_general(left, right, (((0,), (0,)), ((), ())), precision=precisio...  12 us
    all_to_all x1, starting transfers between devices, swapped_in(): shards = lax.all_to_all(shards, axis, split_axis=0, concat_axis=0)  8.75 us
  transfers between devices with their start and end apart: 4, of which 4 were waited for; matrix products, arithmetic and copies ran while one was open for 4% of the time, Pallas kernels for 0%

profile of v1, /device:TPU:2, one launch (start us, length us, event | category | flops | bytes accessed | tf_op | source)
XLA Modules:
  0.0 433.4 jit_solution(2624406265864404248)
XLA Ops:
  7.2 0.8 dynamic-slice_convert_fusion
  7.9 0.1 broadcast_bitcast_fusion
  8.0 1.0 multiply_bitcast_fusion
  9.0 3.4 stack.18
  12.5 8.7 %all-to-all-start = ((f32[16,3,32,1024]{3,2,1,0:T(8,128)}), f32[16,3,32,1024]{3,2,1,0:T(8,128)}, u32[]{:S(2)}, u32[]{:S(2)}) async-start(f32[16,3,32,1024]{3,2,1,0:T(8,128)} %stack.18), calls=%async_computation | async-start | bytes 12582912 | tf_op jit(solution)/shard_map/all_to_all | solution.py:14
  21.2 0.0 reduce-scatter.4.cloned.1.call-start
  21.3 0.3 copy.12
  21.6 4.4 %convolution_subtract_fusion = f32[512,512]{0,1:T(8,128)} fusion(f32[1,512,512]{1,2,0:T(8,128)S(1)} %copy.12, f32[3,512,512]{2,1,0:T(8,128)} %param.8), kind=kOutput, calls=%fused_computation.10 | convolution fusion | flops 1610874880 | bytes 4194304 | tf_op jit(solution)/shard_map/dot_general | solution.py:19
  26.0 134.5 %all-to-all-done = f32[16,3,32,1024]{3,2,1,0:T(8,128)} async-done(((f32[16,3,32,1024]{3,2,1,0:T(8,128)}), f32[16,3,32,1024]{3,2,1,0:T(8,128)}, u32[]{:S(2)}, u32[]{:S(2)}) %all-to-all-start) | async-done | bytes 6291488 | tf_op jit(solution)/shard_map/all_to_all | solution.py:14
  160.5 3.5 fusion.59
  164.0 0.0 copy-start
  164.1 1.9 fusion.62
  166.0 0.7 copy-done
  166.7 2.0 bitcast_add_fusion.2
  168.7 0.0 copy-start.7
  168.7 0.0 copy-start.9
  168.7 2.1 bitcast_add_fusion
  170.8 0.0 copy-done.3
  170.8 0.0 copy-done.7
  170.8 0.8 copy-done.9
  171.6 10.9 %fusion.1 = f32[1536,1024]{1,0:T(8,128)S(1)} fusion(f32[1024,1024]{1,0:T(8,128)S(1)} %copy-done.9, f32[512,1024]{1,0:T(8,128)S(1)} %bitcast_add_fusion, f32[512,1024]{1,0:T(8,128)S(1)} %bitcast_add_fusion.2, f32[512,1024]{1,0:T(8,128)S(1)} %bitcast.101), kind=kOutput, calls=%fused_computation.2 | convolution fusion | flops 9666822144 | bytes 16777216 | tf_op jit(solution)/shard_map/dot_general | solution.py:19
  182.6 3.2 copy.11
  185.8 0.0 reduce-scatter.4.cloned.1.call-update
  185.8 0.0 all-reduce.3.cloned.1.call-start
  185.9 1.2 bitcast_negate_fusion
  187.1 2.0 fusion.18
  189.1 1.0 fusion.63
  190.1 81.5 %reduce-scatter.4.cloned.1.call-done = f32[3,1,32,1024]{3,2,0,1:T(8,128)} async-done(((f32[3,16,32,1024]{3,2,0,1:T(8,128)}), f32[3,1,32,1024]{3,2,0,1:T(8,128)}) %reduce-scatter.4.cloned.1.call-update) | async-done | bytes 393232
  271.7 5.0 %collective-permute-start = (f32[3,32,1024]{2,1,0:T(8,128)}, f32[3,32,1024]{2,1,0:T(8,128)S(1)}, u32[]{:S(2)}, u32[]{:S(2)}) collective-permute-start(f32[3,32,1024]{2,1,0:T(8,128)} %bitcast.107), channel_id=1, source_target_pairs={{0,0},{1,16},{2,32},{3,48},{4,64},{5,80},{6,96},{7,112},{8,128},{9... | collective-permute-start | bytes 1179656 | tf_op jit(solution)/shard_map/ppermute | solution.py:64
  276.6 2.0 fusion.16
  278.6 3.7 fusion.60
  282.4 29.7 %collective-permute-done = f32[3,32,1024]{2,1,0:T(8,128)S(1)} collective-permute-done((f32[3,32,1024]{2,1,0:T(8,128)}, f32[3,32,1024]{2,1,0:T(8,128)S(1)}, u32[]{:S(2)}, u32[]{:S(2)}) %collective-permute-start) | collective-permute-done | bytes 393248 | tf_op jit(solution)/shard_map/ppermute | solution.py:64
  312.1 0.8 fusion.61
  312.9 3.0 fusion
  315.8 2.0 fusion.2
  317.9 1.1 fusion.38
  318.9 0.8 pad_maximum_fusion.3
  319.7 0.0 all-reduce.3.cloned.1.call-update
  319.7 2.1 fusion.14
  321.8 2.3 convolution_add_fusion.1
  324.1 92.2 %all-reduce.3.cloned.1.call-done = f32[32,3072]{1,0:T(8,128)} async-done(((f32[32,3072]{1,0:T(8,128)}), f32[32,3072]{1,0:T(8,128)}) %all-reduce.3.cloned.1.call-update) | async-done | bytes 393232 | tf_op jit(solution)/shard_map/psum | solution.py:68
  416.2 2.3 fusion.12
  418.5 1.6 fusion.13
  420.1 0.9 fusion.39
  421.0 1.6 fusion.9
  422.6 1.6 fusion.11
  424.2 1.6 fusion.7
  425.8 0.8 pad_maximum_fusion.4
  (16 shorter events, 0.0 us)
Async XLA Ops:
  12.5 8.8 %slice-start = ((f32[3,512,512]{2,1,0:T(8,128)}), f32[1,512,512]{2,1,0:T(8,128)S(1)}, s32[]{:S(2)}) async-start(f32[3,512,512]{2,1,0:T(8,128)} %param.8), calls=%async_computation.4 | async-start | bytes 2097152 | tf_op jit(solution)/shard_map/slice | solution.py:53
  12.5 148.0 %all-to-all-start = ((f32[16,3,32,1024]{3,2,1,0:T(8,128)}), f32[16,3,32,1024]{3,2,1,0:T(8,128)}, u32[]{:S(2)}, u32[]{:S(2)}) async-start(f32[16,3,32,1024]{3,2,1,0:T(8,128)} %stack.18), calls=%async_computation | async-start | bytes 12582912 | tf_op jit(solution)/shard_map/all_to_all | solution.py:14
  21.2 250.4 %reduce-scatter.4.cloned.1.call-start = ((), (), s32[]{:S(2)}) async-start(), calls=%async_computation.3 | async-start | bytes 6684672
  160.5 3.6 copy-start.1
  164.0 6.7 %copy-start.3 = (f32[1,16,32,1024]{3,2,0,1:T(8,128)}, f32[1,16,32,1024]{3,2,0,1:T(8,128)S(1)}, u32[]{:S(2)}) copy-start(f32[1,16,32,1024]{3,2,0,1:T(8,128)S(1)} %get-tuple-element.5) | copy-start | bytes 6291460
  164.0 2.6 copy-start
  168.7 2.1 copy-start.7
  168.7 2.9 copy-start.9
  171.6 10.9 %copy-start.5 = (f32[512,1024]{1,0:T(8,128)}, f32[512,1024]{1,0:T(8,128)S(1)}, u32[]{:S(2)}) copy-start(f32[512,1024]{1,0:T(8,128)S(1)} %bitcast_add_fusion) | copy-start | bytes 6291460
  185.8 230.4 %all-reduce.3.cloned.1.call-start = ((), (), s32[]{:S(2)}) async-start(), calls=%async_computation.2 | async-start | bytes 786432 | tf_op jit(solution)/shard_map/psum | solution.py:68
  185.9 3.2 copy-start.2
  271.7 40.4 %collective-permute-start = (f32[3,32,1024]{2,1,0:T(8,128)}, f32[3,32,1024]{2,1,0:T(8,128)S(1)}, u32[]{:S(2)}, u32[]{:S(2)}) collective-permute-start(f32[3,32,1024]{2,1,0:T(8,128)} %bitcast.107), channel_id=1, source_target_pairs={{0,0},{1,16},{2,32},{3,48},{4,64},{5,80},{6,96},{7,112},{8,128},{9... | collective-permute-start | bytes 1179656 | tf_op jit(solution)/shard_map/ppermute | solution.py:64
  278.6 34.3 %copy-start.4 = (f32[1,16,32,1024]{3,2,0,1:T(8,128)S(1)}, f32[1,16,32,1024]{3,2,0,1:T(8,128)}, u32[]{:S(2)}) copy-start(f32[1,16,32,1024]{3,2,0,1:T(8,128)} %copy-done.3) | copy-start | bytes 6291460
  278.6 34.3 %copy-start.6 = (f32[512,1024]{1,0:T(8,128)S(1)}, f32[512,1024]{1,0:T(8,128)}, u32[]{:S(2)}) copy-start(f32[512,1024]{1,0:T(8,128)} %copy-done.5) | copy-start | bytes 6291460
  278.6 34.2 %copy-start.8 = (f32[512,1024]{1,0:T(8,128)S(1)}, f32[512,1024]{1,0:T(8,128)}, u32[]{:S(2)}) copy-start(f32[512,1024]{1,0:T(8,128)} %copy-done.7) | copy-start | bytes 6291460
Sparse Core Ops, SparseCore 0:
  185.9 85.6 reduce-scatter.3
  319.9 96.3 all-reduce.2
